TPU v7x, 32 devices: a whole 2x2x4 slice. The times are simulated.
32 devices in a mesh: dp: 8 (over z, x), tensor: 4 (over y, core).
Axes of the slice: x: 2, y: 2, z: 4, core: 2. Of those that a mesh axis runs over, the one named last changes fastest.
Arguments:
- layer_in: bfloat16 [16384, 1024], P(('dp', 'tensor')), may hold values from -6 to 6
- cotangent: bfloat16 [16384, 1024], P(('dp', 'tensor')), may hold values from -6 to 6
- lengths: int32 [8], P('dp'), may hold values from 256 to 2048, as said below
- languages: int32 [8], P('dp'), may hold values from 0 to 45
- lang_weight: float32 [46], replicated, may hold values from 0.3 to 3
- ln1_gain: float32 [1024], replicated, may hold values from 0.5 to 1.5
- ln1_bias: float32 [1024], replicated, may hold values from -2.5 to 2.5
- w_qkv: bfloat16 [1024, 3072], P(None, 'tensor'), may hold values from -0.1875 to 0.1875
- b_qv: float32 [2048], P('tensor'), may hold values from -2.5 to 2.5
- w_out: bfloat16 [1024, 1024], P('tensor'), may hold values from -1.5 to 1.5
- b_out: float32 [1024], replicated, may hold values from -2.5 to 2.5
- ln2_gain: float32 [1024], replicated, may hold values from 0.5 to 1.5
- ln2_bias: float32 [1024], replicated, may hold values from -2.5 to 2.5
- w_up: bfloat16 [1024, 4096], P(None, 'tensor'), may hold values from -0.1875 to 0.1875
- b_up: float32 [4096], P('tensor'), may hold values from -2.5 to 2.5
- w_down: bfloat16 [4096, 1024], P('tensor'), may hold values from -0.09375 to 0.09375
- b_down: float32 [1024], replicated, may hold values from -2.5 to 2.5
Outputs:
- output: bfloat16 [16384, 1024], P(('dp', 'tensor'))
- grad_x: bfloat16 [16384, 1024], P(('dp', 'tensor'))
- g_ln1_gain: float32 [1024], replicated
- g_ln1_bias: float32 [1024], replicated
- g_w_qkv: float32 [1024, 3072], P(None, 'tensor')
- g_b_qv: float32 [2048], P('tensor')
- g_w_out: float32 [1024, 1024], P('tensor')
- g_b_out: float32 [1024], replicated
- g_ln2_gain: float32 [1024], replicated
- g_ln2_bias: float32 [1024], replicated
- g_w_up: float32 [1024, 4096], P(None, 'tensor')
- g_b_up: float32 [4096], P('tensor')
- g_w_down: float32 [4096, 1024], P('tensor')
- g_b_down: float32 [1024], replicated
Inputs may be any that keep to these rules, and one draw needn't show every extreme that they name: `lengths`: rows of languages 0 to 7 have all 2048 tokens; some row has 2048 tokens and some row 256.
All inputs are finite; a program needn't handle non-finite values.
Results may differ from a plain program's by a relative error of at most 0.019.
Values may be sent and summed in bfloat16 or wider, within the bound.
No kernel may reach another device: no remote copies, remote signals or barrier semaphores. Data moves between devices by JAX's collectives and lax.ppermute only.
A program may use at most 192 MiB of HBM per device.

v0:
```python
import jax
import jax.numpy as jnp
from jax import lax
from jax.sharding import PartitionSpec as P

HEADS = 16
HD = 64
eps = 1e-05
block_most = 512


def layer_norm(values, gain, bias):
    centre = jnp.mean(values, axis=-1, keepdims=True)
    shifted = values - centre
    spread = jnp.mean(shifted * shifted, axis=-1, keepdims=True)
    factor = lax.rsqrt(spread + eps)
    unit_rows = shifted * factor
    return (unit_rows * gain + bias, unit_rows, factor)


def norm_back(grad_rows, unit_rows, factor, gain):
    scaled = grad_rows * gain
    inner = jnp.mean(scaled * unit_rows, axis=-1, keepdims=True)
    return factor * (scaled - jnp.mean(scaled, axis=-1, keepdims=True) - unit_rows * inner)


def cross_rows(left, right):
    return lax.dot_general(
        left, right, (((0,), (0,)), ((), ())), preferred_element_type=jnp.float32
    )


def times_trans(left, right):
    return lax.dot_general(
        left, right, (((1,), (1,)), ((), ())), preferred_element_type=jnp.float32
    )


def block_rows():
    return block_most


def qkv_bias(pairs):
    return jnp.stack([pairs[:, 0], jnp.zeros_like(pairs[:, 0]), pairs[:, 1]], axis=1)


def masked_scores(query_block, keys, start, length, slopes):
    query_pos = start + jnp.arange(query_block.shape[1], dtype=jnp.int32)
    key_pos = jnp.arange(keys.shape[1], dtype=jnp.int32)
    scores = jnp.einsum(
        "hqe,hke->hqk", query_block, keys, preferred_element_type=jnp.float32
    ) * keys.shape[2] ** (-0.5)
    offsets = (key_pos[None, :] - query_pos[:, None]).astype(jnp.float32)
    scores = scores + slopes[:, None, None] * offsets[None]
    allowed = (key_pos[None, :] <= query_pos[:, None]) & (key_pos[None, :] < length)
    return jnp.where(allowed[None], scores, -jnp.inf)


def attend_forward(query, keys, values, length, slopes):
    span = query.shape[1]
    block = block_rows()

    def forward_block(start):
        query_block = lax.dynamic_slice_in_dim(query, start, block, 1)
        scores = masked_scores(query_block, keys, start, length, slopes)
        highest = jnp.max(scores, axis=-1, keepdims=True)
        expos = jnp.exp(scores - highest)
        denom = jnp.sum(expos, axis=-1, keepdims=True)
        probs_b = (expos / denom).astype(jnp.bfloat16)
        result = jnp.einsum("hqk,hke->hqe", probs_b, values, preferred_element_type=jnp.float32)
        return (result, (highest + jnp.log(denom))[..., 0])

    starts = jnp.arange(span // block, dtype=jnp.int32) * block
    results, log_total = lax.map(forward_block, starts)
    heads_count = query.shape[0]
    return (
        results.transpose(1, 0, 2, 3).reshape(query.shape),
        log_total.transpose(1, 0, 2).reshape(heads_count, span),
    )


def attend_backward(query, keys, values, grad_heads, log_total, length, slopes):
    span = query.shape[1]
    block = block_rows()
    scale = keys.shape[2] ** (-0.5)

    def backward_block(carry, start):
        grad_keys, grad_values = carry
        query_block = lax.dynamic_slice_in_dim(query, start, block, 1)
        grad_block = lax.dynamic_slice_in_dim(grad_heads, start, block, 1)
        log_block = lax.dynamic_slice_in_dim(log_total, start, block, 1)
        scores = masked_scores(query_block, keys, start, length, slopes)
        probs = jnp.exp(scores - log_block[..., None])
        grad_probs = jnp.einsum(
            "hqe,hke->hqk", grad_block, values, preferred_element_type=jnp.float32
        )
        grad_scores = (
            probs * (grad_probs - jnp.sum(probs * grad_probs, axis=-1, keepdims=True))
        ).astype(jnp.bfloat16)
        grad_query = (
            jnp.einsum("hqk,hke->hqe", grad_scores, keys, preferred_element_type=jnp.float32)
            * scale
        )
        grad_keys = (
            grad_keys
            + jnp.einsum(
                "hqk,hqe->hke", grad_scores, query_block, preferred_element_type=jnp.float32
            )
            * scale
        )
        grad_values = grad_values + jnp.einsum(
            "hqk,hqe->hke",
            probs.astype(jnp.bfloat16),
            grad_block,
            preferred_element_type=jnp.float32,
        )
        return ((grad_keys, grad_values), grad_query)

    starts = jnp.arange(span // block, dtype=jnp.int32) * block
    empty = jnp.zeros(keys.shape, jnp.float32)
    (grad_keys, grad_values), grad_query = lax.scan(backward_block, (empty, empty), starts)
    return (grad_query.transpose(1, 0, 2, 3).reshape(query.shape), grad_keys, grad_values)


def body(
    layer_in,
    cotangent,
    lengths,
    languages,
    lang_weight,
    ln1_gain,
    ln1_bias,
    w_qkv,
    b_qv,
    w_out,
    b_out,
    ln2_gain,
    ln2_bias,
    w_up,
    b_up,
    w_down,
    b_down,
):
    groups = lax.axis_size("tensor")
    place = lax.axis_index("tensor")
    own_rows = layer_in.shape[0]
    all_rows = own_rows * groups
    seq_count = lengths.shape[0]
    seq_len = all_rows // seq_count
    head_dim = HD
    local_heads = w_out.shape[0] // head_dim
    head_ids = (place * local_heads + jnp.arange(local_heads, dtype=jnp.int32)).astype(jnp.float32)
    slopes = jnp.exp2(-8.0 * (head_ids + 1.0) / HEADS)
    in_float = layer_in.astype(jnp.float32)
    normed1, unit1, factor1 = layer_norm(in_float, ln1_gain, ln1_bias)
    normed1_b = normed1.astype(jnp.bfloat16)
    mixed = jnp.dot(
        lax.all_gather(normed1_b, "tensor", axis=0, tiled=True),
        w_qkv,
        preferred_element_type=jnp.float32,
    )
    bias_three = qkv_bias(b_qv.reshape(local_heads, 2, head_dim))
    mixed_b = (mixed.reshape(all_rows, local_heads, 3, head_dim) + bias_three[None]).astype(
        jnp.bfloat16
    )
    per_seq = mixed_b.reshape(seq_count, seq_len, local_heads, 3, head_dim).transpose(0, 3, 2, 1, 4)

    def forward_seq(item):
        parts, length = item
        return attend_forward(parts[0], parts[1], parts[2], length, slopes)

    heads_out, log_total = lax.map(forward_seq, (per_seq, lengths))
    heads_b = (
        heads_out.astype(jnp.bfloat16)
        .transpose(0, 2, 1, 3)
        .reshape(all_rows, local_heads * head_dim)
    )
    attn_sum = lax.psum_scatter(
        jnp.dot(heads_b, w_out, preferred_element_type=jnp.float32).astype(jnp.bfloat16),
        "tensor",
        scatter_dimension=0,
        tiled=True,
    ).astype(jnp.float32)
    middle = in_float + attn_sum + b_out
    normed2, unit2, factor2 = layer_norm(middle, ln2_gain, ln2_bias)
    normed2_b = normed2.astype(jnp.bfloat16)
    pre_act = (
        jnp.dot(
            lax.all_gather(normed2_b, "tensor", axis=0, tiled=True),
            w_up,
            preferred_element_type=jnp.float32,
        )
        + b_up
    )
    gelu_out, gelu_pull = jax.vjp(lambda inputs: jax.nn.gelu(inputs, approximate=True), pre_act)
    active_b = gelu_out.astype(jnp.bfloat16)
    output = (
        middle
        + lax.psum_scatter(
            jnp.dot(active_b, w_down, preferred_element_type=jnp.float32).astype(jnp.bfloat16),
            "tensor",
            scatter_dimension=0,
            tiled=True,
        ).astype(jnp.float32)
        + b_down
    )
    row_ids = place * own_rows + jnp.arange(own_rows, dtype=jnp.int32)
    seq_ids = row_ids // seq_len
    positions = row_ids - seq_ids * seq_len
    seq_hit = seq_ids[:, None] == jnp.arange(seq_count, dtype=jnp.int32)[None, :]
    row_length = jnp.sum(jnp.where(seq_hit, lengths[None, :], 0), axis=1)
    row_lang = jnp.sum(jnp.where(seq_hit, languages[None, :], 0), axis=1)
    lang_hit = row_lang[:, None] == jnp.arange(lang_weight.shape[0], dtype=jnp.int32)[None, :]
    row_weight = jnp.sum(jnp.where(lang_hit, lang_weight[None, :], 0.0), axis=1)
    live = jnp.where(positions < row_length, row_weight, 0.0)
    grad_top = cotangent.astype(jnp.float32) * live[:, None]
    g_b_down = jnp.sum(grad_top, axis=0)
    grad_full = lax.all_gather(grad_top.astype(jnp.bfloat16), "tensor", axis=0, tiled=True)
    g_w_down = cross_rows(active_b, grad_full)
    grad_active = times_trans(grad_full, w_down)
    grad_pre_b = gelu_pull(grad_active)[0].astype(jnp.bfloat16)
    g_b_up = jnp.sum(grad_pre_b.astype(jnp.float32), axis=0)
    rows_here = grad_pre_b
    g_w_up = cross_rows(lax.all_gather(normed2_b, "tensor", axis=0, tiled=True), rows_here)
    grad_norm2 = lax.psum_scatter(
        times_trans(grad_pre_b, w_up).astype(jnp.bfloat16),
        "tensor",
        scatter_dimension=0,
        tiled=True,
    ).astype(jnp.float32)
    g_ln2_gain = jnp.sum(grad_norm2 * unit2, axis=0)
    g_ln2_bias = jnp.sum(grad_norm2, axis=0)
    grad_middle = grad_top + norm_back(grad_norm2, unit2, factor2, ln2_gain)
    g_b_out = jnp.sum(grad_middle, axis=0)
    grad_mid_b = grad_middle.astype(jnp.bfloat16)
    grad_mid_full = lax.all_gather(grad_mid_b, "tensor", axis=0, tiled=True)
    g_w_out = cross_rows(heads_b, grad_mid_full)
    grad_heads_b = times_trans(grad_mid_full, w_out).astype(jnp.bfloat16)
    grad_seq = grad_heads_b.reshape(seq_count, seq_len, local_heads, head_dim).transpose(0, 2, 1, 3)

    def backward_seq(item):
        parts, grad_part, log_part, length = item
        return attend_backward(parts[0], parts[1], parts[2], grad_part, log_part, length, slopes)

    grad_query, grad_key, grad_value = lax.map(
        backward_seq, (per_seq, grad_seq, log_total, lengths)
    )
    grad_parts = jnp.stack([grad_query, grad_key, grad_value], axis=1)
    grad_mixed_b = (
        grad_parts.transpose(0, 3, 2, 1, 4)
        .reshape(all_rows, local_heads * 3 * head_dim)
        .astype(jnp.bfloat16)
    )
    column_sums = jnp.sum(grad_mixed_b.astype(jnp.float32), axis=0).reshape(
        local_heads, 3, head_dim
    )
    g_b_qv = jnp.stack([column_sums[:, 0], column_sums[:, 2]], axis=1).reshape(-1)
    rows_here = grad_mixed_b
    g_w_qkv = cross_rows(lax.all_gather(normed1_b, "tensor", axis=0, tiled=True), rows_here)
    grad_norm1 = lax.psum_scatter(
        times_trans(grad_mixed_b, w_qkv).astype(jnp.bfloat16),
        "tensor",
        scatter_dimension=0,
        tiled=True,
    ).astype(jnp.float32)
    g_ln1_gain = jnp.sum(grad_norm1 * unit1, axis=0)
    g_ln1_bias = jnp.sum(grad_norm1, axis=0)
    grad_input = grad_middle + norm_back(grad_norm1, unit1, factor1, ln1_gain)
    weights = (
        lax.psum(g_w_qkv.astype(jnp.bfloat16), "dp").astype(jnp.float32),
        lax.psum(g_b_qv.astype(jnp.bfloat16), "dp").astype(jnp.float32),
        lax.psum(g_w_out.astype(jnp.bfloat16), "dp").astype(jnp.float32),
        lax.psum(g_w_up.astype(jnp.bfloat16), "dp").astype(jnp.float32),
        lax.psum(g_b_up.astype(jnp.bfloat16), "dp").astype(jnp.float32),
        lax.psum(g_w_down.astype(jnp.bfloat16), "dp").astype(jnp.float32),
    )
    shared = lax.psum(
        (g_ln1_gain, g_ln1_bias, g_b_out, g_ln2_gain, g_ln2_bias, g_b_down), ("dp", "tensor")
    )
    return (
        output.astype(jnp.bfloat16),
        grad_input.astype(jnp.bfloat16),
        shared[0],
        shared[1],
        weights[0],
        weights[1],
        weights[2],
        shared[2],
        shared[3],
        shared[4],
        weights[3],
        weights[4],
        weights[5],
        shared[5],
    )


def solution(mesh):
    in_specs = (
        P(("dp", "tensor"), None),
        P(("dp", "tensor"), None),
        P("dp"),
        P("dp"),
        P(),
        P(),
        P(),
        P(None, "tensor"),
        P("tensor"),
        P("tensor", None),
        P(),
        P(),
        P(),
        P(None, "tensor"),
        P("tensor"),
        P("tensor", None),
        P(),
    )
    out_specs = (
        P(("dp", "tensor"), None),
        P(("dp", "tensor"), None),
        P(),
        P(),
        P(None, "tensor"),
        P("tensor"),
        P("tensor", None),
        P(),
        P(),
        P(),
        P(None, "tensor"),
        P("tensor"),
        P("tensor", None),
        P(),
    )
    return jax.shard_map(body, mesh=mesh, in_specs=in_specs, out_specs=out_specs, check_vma=False)
```

profile of v0, /device:TPU:0, one launch (start us, length us, event | category | flops | bytes accessed | tf_op | source)
XLA Modules:
  0.0 1035.9 jit_solution(2467794752946454012)
XLA Ops:
  14.1 37.0 %all-gather.5.cloned.1.call-done = bf16[2048,1024]{1,0:T(8,128)(2,1)} async-done(((bf16[512,1024]{1,0:T(8,128)(2,1)}), bf16[2048,1024]{1,0:T(8,128)(2,1)}) %all-gather.5.cloned.1.call-update) | async-done | bytes 4194320 | tf_op jit(solution)/shard_map/all_gather | solution.py:158
  60.2 106.7 %while.48 = (s32[]{:T(128)}, bf16[4,4,512,64]{2,3,1,0:T(8,128)(2,1)}, f32[4,4,512]{2,1,0:T(4,128)S(1)}, s32[4]{0:T(128)S(1)}, s32[]{:T(128)}, /*index=5*/bf16[4,...) while((s32[]{:T(128)}, ...), condition=%wide.region_5.6_spmd.clone, body=%wide.region_2.5_spmd.clone.sunk | while | flops 1153434112 | bytes 99428696 | solution.py:74
  177.4 44.6 %reduce-scatter.5.cloned.1.call-done = bf16[512,1024]{1,0:T(8,128)(2,1)} async-done(((bf16[2048,1024]{1,0:T(8,128)(2,1)}), bf16[512,1024]{1,0:T(8,128)(2,1)}) %reduce-scatter.5.cloned.1.call-update) | async-done | bytes 1048592 | tf_op jit(solution)/shard_map/reduce_scatter | solution.py:178
  231.2 30.6 %all-gather.7.cloned.1.call-done = bf16[2048,1024]{1,0:T(8,128)(2,1)} async-done(((bf16[512,1024]{1,0:T(8,128)(2,1)}), bf16[2048,1024]{1,0:T(8,128)(2,1)}) %all-gather.7.cloned.1.call-update) | async-done | bytes 4194320 | tf_op jit(solution)/shard_map/all_gather | solution.py:189
  261.8 11.4 %fusion.83 = f32[2048,1024]{1,0:T(8,128)} fusion(bf16[2048,1024]{1,0:T(8,128)(2,1)} %all-gather.7.cloned.1.call-done, bf16[1024,1024]{1,0:T(8,128)(2,1)} %param.34), kind=kOutput, calls=%fused_computation.151 | convolution fusion | flops 4294967296 | bytes 14680064 | tf_op jit(solution)/shard_map/dot_general | solution.py:188
  273.2 25.2 %all-gather.9.cloned.1.call-done = bf16[2048,1024]{1,0:T(8,128)(2,1)} async-done(((bf16[512,1024]{1,0:T(8,128)(2,1)}), bf16[2048,1024]{1,0:T(8,128)(2,1)}) %all-gather.9.cloned.1.call-update) | async-done | bytes 4194320 | tf_op jit(solution)/shard_map/all_gather | solution.py:218
  298.4 13.8 %fusion.76 = (bf16[1024]{0:T(1024)(128)(2,1)}, bf16[2048,1024]{1,0:T(8,128)(2,1)S(1)}) fusion(f32[2048,1024]{1,0:T(8,128)} %fusion.83, f32[1024]{0:T(1024)S(1)} %copy-done.50, bf16[2048,1024]{1,0:T(8,128)(2,1)} %all-gather.9.cloned.1.call-done, bf16[1024,1024]{1,0:T(8,128)(2,1)S(1)} %copy-done), kind=kOutput, calls=%fused_computation.146 | convolution fusion | flops 4341103616 | bytes 18880512 | tf_op jit(solution)/shard_map/dot_general | solution.py:34
  320.4 11.2 %convolution_convert_fusion.3 = bf16[2048,1024]{1,0:T(8,128)(2,1)} fusion(bf16[1024,1024]{1,0:T(8,128)(2,1)S(1)} %copy-done, f32[2048,1024]{1,0:T(8,128)} %fusion.83, f32[1024]{0:T(1024)S(1)} %copy-done.50), kind=kOutput, calls=%fused_computation.65 | convolution fusion | flops 4318035968 | bytes 14684160 | tf_op jit(solution)/shard_map/dot_general | solution.py:200
  331.7 33.4 %reduce-scatter.9.cloned.1.call-done = bf16[512,1024]{1,0:T(8,128)(2,1)} async-done(((bf16[2048,1024]{1,0:T(8,128)(2,1)}), bf16[512,1024]{1,0:T(8,128)(2,1)}) %reduce-scatter.9.cloned.1.call-update) | async-done | bytes 1048592 | tf_op jit(solution)/shard_map/reduce_scatter | solution.py:225
  368.1 44.5 %reduce-scatter.7.cloned.1.call-done = bf16[512,1024]{1,0:T(8,128)(2,1)} async-done(((bf16[2048,1024]{1,0:T(8,128)(2,1)}), bf16[512,1024]{1,0:T(8,128)(2,1)}) %reduce-scatter.7.cloned.1.call-update) | async-done | bytes 1048592 | tf_op jit(solution)/shard_map/reduce_scatter | solution.py:199
  440.1 14.0 %all-gather.11.cloned.1.call-done = bf16[2048,1024]{1,0:T(8,128)(2,1)} async-done(((bf16[512,1024]{1,0:T(8,128)(2,1)}), bf16[2048,1024]{1,0:T(8,128)(2,1)}) %all-gather.11.cloned.1.call-update) | async-done | bytes 4194320 | tf_op jit(solution)/shard_map/all_gather | solution.py:236
  459.6 244.7 %while.49 = (s32[]{:T(128)}, f32[4,2048,64]{1,2,0:T(8,128)}, f32[4,2048,64]{1,2,0:T(8,128)}, bf16[4,4,512,64]{2,3,1,0:T(8,128)(2,1)}, s32[4]{0:T(128)S(1)}, /*in...) while((s32[]{:T(128)}, f32[4,2048,64]{1,2,0:T(8,128)}, ...), condition=%wide.region_16.17_spmd.clone, body=%wide.region_14.16_spmd.clone.sunk | while | flops 2737439232 | bytes 296274944 | solution.py:121
  474.2 14.5 %multiply_reduce_fusion.3 = (f32[4,512]{1,0:T(4,128)S(1)}, f32[4,512,2048]{2,1,0:T(8,128)}) fusion(f32[4,512,2048]{2,1,0:T(8,128)} %fusion.148, f32[4,512]{1,0:T(4,128)S(1)} %constant_dynamic-slice_fusion.2, f32[512,2048]{1,0:T(8,128)S(1)} %subtract_convert_fusion.5, f32[4]{0:T(128)S(1)} %multiply_exponential_fusion.5, ...), kind=kOutput, calls=%fused_computation.23.clone.1 | convolution fusion | flops 566228992 | bytes 40124932 | tf_op jit(solution)/shard_map/while/body/eval_jaxpr/while/body/eval_jaxpr/hqe,hke->hqk/dot_general | solution.py:50
  488.6 15.0 %multiply_convert_fusion.5 = bf16[4,512,2048]{2,1,0:T(8,128)(2,1)} fusion(f32[4,512,2048]{2,1,0:T(8,128)} %get-tuple-element.456, f32[4,512,2048]{2,1,0:T(8,128)} %fusion.148, f32[4,512]{1,0:T(4,128)S(1)} %get-tuple-element.457), kind=kLoop, calls=%fused_computation.22.clone.1 | loop fusion | flops 12582912 | bytes 41951232 | tf_op jit(solution)/shard_map/while/body/eval_jaxpr/while/body/eval_jaxpr/convert_element_type | solution.py:99
  535.2 14.5 %multiply_reduce_fusion.3 = (f32[4,512]{1,0:T(4,128)S(1)}, f32[4,512,2048]{2,1,0:T(8,128)}) fusion(f32[4,512,2048]{2,1,0:T(8,128)} %fusion.148, f32[4,512]{1,0:T(4,128)S(1)} %constant_dynamic-slice_fusion.2, f32[512,2048]{1,0:T(8,128)S(1)} %subtract_convert_fusion.5, f32[4]{0:T(128)S(1)} %multiply_exponential_fusion.5, ...), kind=kOutput, calls=%fused_computation.23.clone.1 | convolution fusion | flops 566228992 | bytes 40124932 | tf_op jit(solution)/shard_map/while/body/eval_jaxpr/while/body/eval_jaxpr/hqe,hke->hqk/dot_general | solution.py:50
  549.7 15.0 %multiply_convert_fusion.5 = bf16[4,512,2048]{2,1,0:T(8,128)(2,1)} fusion(f32[4,512,2048]{2,1,0:T(8,128)} %get-tuple-element.456, f32[4,512,2048]{2,1,0:T(8,128)} %fusion.148, f32[4,512]{1,0:T(4,128)S(1)} %get-tuple-element.457), kind=kLoop, calls=%fused_computation.22.clone.1 | loop fusion | flops 12582912 | bytes 41951232 | tf_op jit(solution)/shard_map/while/body/eval_jaxpr/while/body/eval_jaxpr/convert_element_type | solution.py:99
  596.3 14.5 %multiply_reduce_fusion.3 = (f32[4,512]{1,0:T(4,128)S(1)}, f32[4,512,2048]{2,1,0:T(8,128)}) fusion(f32[4,512,2048]{2,1,0:T(8,128)} %fusion.148, f32[4,512]{1,0:T(4,128)S(1)} %constant_dynamic-slice_fusion.2, f32[512,2048]{1,0:T(8,128)S(1)} %subtract_convert_fusion.5, f32[4]{0:T(128)S(1)} %multiply_exponential_fusion.5, ...), kind=kOutput, calls=%fused_computation.23.clone.1 | convolution fusion | flops 566228992 | bytes 40124932 | tf_op jit(solution)/shard_map/while/body/eval_jaxpr/while/body/eval_jaxpr/hqe,hke->hqk/dot_general | solution.py:50
  610.8 15.0 %multiply_convert_fusion.5 = bf16[4,512,2048]{2,1,0:T(8,128)(2,1)} fusion(f32[4,512,2048]{2,1,0:T(8,128)} %get-tuple-element.456, f32[4,512,2048]{2,1,0:T(8,128)} %fusion.148, f32[4,512]{1,0:T(4,128)S(1)} %get-tuple-element.457), kind=kLoop, calls=%fused_computation.22.clone.1 | loop fusion | flops 12582912 | bytes 41951232 | tf_op jit(solution)/shard_map/while/body/eval_jaxpr/while/body/eval_jaxpr/convert_element_type | solution.py:99
  657.4 14.5 %multiply_reduce_fusion.3 = (f32[4,512]{1,0:T(4,128)S(1)}, f32[4,512,2048]{2,1,0:T(8,128)}) fusion(f32[4,512,2048]{2,1,0:T(8,128)} %fusion.148, f32[4,512]{1,0:T(4,128)S(1)} %constant_dynamic-slice_fusion.2, f32[512,2048]{1,0:T(8,128)S(1)} %subtract_convert_fusion.5, f32[4]{0:T(128)S(1)} %multiply_exponential_fusion.5, ...), kind=kOutput, calls=%fused_computation.23.clone.1 | convolution fusion | flops 566228992 | bytes 40124932 | tf_op jit(solution)/shard_map/while/body/eval_jaxpr/while/body/eval_jaxpr/hqe,hke->hqk/dot_general | solution.py:50
  671.8 15.0 %multiply_convert_fusion.5 = bf16[4,512,2048]{2,1,0:T(8,128)(2,1)} fusion(f32[4,512,2048]{2,1,0:T(8,128)} %get-tuple-element.456, f32[4,512,2048]{2,1,0:T(8,128)} %fusion.148, f32[4,512]{1,0:T(4,128)S(1)} %get-tuple-element.457), kind=kLoop, calls=%fused_computation.22.clone.1 | loop fusion | flops 12582912 | bytes 41951232 | tf_op jit(solution)/shard_map/while/body/eval_jaxpr/while/body/eval_jaxpr/convert_element_type | solution.py:99
  731.0 22.5 %all-reduce.1 = (bf16[512]{0:T(512)(128)(2,1)S(1)}, bf16[1024]{0:T(1024)(128)(2,1)S(1)}) all-reduce(bf16[512]{0:T(512)(128)(2,1)S(1)} %convert_element_type.190, bf16[1024]{0:T(1024)(128)(2,1)S(1)} %copy-done.43), channel_id=1, replica_groups=mesh['dp'=8,'tensor'=4] {'dp'}, use_global_device_ids=true, to_apply=%region_26.27 | all-reduce | flops 1536 | bytes 6144 | tf_op jit(solution)/shard_map/psum | solution.py:271
  754.7 182.3 %all-reduce.5.cloned.1.call-done = (bf16[1024,768]{1,0:T(8,128)(2,1)}, bf16[256,1024]{1,0:T(8,128)(2,1)}, bf16[1024,1024]{1,0:T(8,128)(2,1)}, bf16[1024,1024]{1,0:T(8,128)(2,1)}) async-done(((bf16[1024,768]{1,0:T(8,128)(2,1)}, bf16[256,1024]{1,0:T(8,128)(2,1)}, bf16[1024,1024]{1,0:T(8,128)(2,1)}, bf16[1024,1024]{1,0:T(8,128)(2,1)}), (bf16[1024,768]{1,0:T(8,128)(2,1)}, bf16[256,1024]{1,0:T(8,128)(2,1)}, ...) | async-done | bytes 6291472 | tf_op jit(solution)/shard_map/psum | solution.py:270
  947.9 35.0 %reduce-scatter.11.cloned.1.call-done = bf16[512,1024]{1,0:T(8,128)(2,1)} async-done(((bf16[2048,1024]{1,0:T(8,128)(2,1)}), bf16[512,1024]{1,0:T(8,128)(2,1)}) %reduce-scatter.11.cloned.1.call-update) | async-done | bytes 1048592 | tf_op jit(solution)/shard_map/reduce_scatter | solution.py:260
  985.3 40.0 %all-reduce = (f32[1024]{0:T(1024)}, f32[1024]{0:T(1024)}, f32[1024]{0:T(1024)}, f32[1024]{0:T(1024)}, f32[1024]{0:T(1024)}, /*index=5*/f32[1024]{0:T(1024)}) all-reduce(f32[1024]{0:T(1024)S(1)} %get-tuple-element.241, f32[1024]{0:T(1024)S(1)} %get-tuple-element.246, ...), channel_id=1, replica_groups=mesh['dp'=8,'tensor'=4] {'dp','tensor'}, use_global_device_ids=true, to_apply=%region_21.22 | all-reduce | flops 6144 | bytes 49152 | tf_op jit(solution)/shard_map/psum | solution.py:277
  (338 shorter events, 339.4 us)
Async XLA Ops:
  7.2 291.2 %copy-start = (bf16[1024,1024]{1,0:T(8,128)(2,1)S(1)}, bf16[1024,1024]{1,0:T(8,128)(2,1)}, u32[]{:S(2)}) copy-start(bf16[1024,1024]{1,0:T(8,128)(2,1)} %param.36) | copy-start | bytes 6291460
  7.2 43.9 %all-gather.5.cloned.1.call-start = ((), (), s32[]{:S(2)}) async-start(), calls=%async_computation.4 | async-start | bytes 5242880 | tf_op jit(solution)/shard_map/all_gather | solution.py:158
  13.8 208.2 %reduce-scatter.5.cloned.1.call-start = ((), (), s32[]{:S(2)}) async-start(), calls=%async_computation.5 | async-start | bytes 5242880 | tf_op jit(solution)/shard_map/reduce_scatter | solution.py:178
  177.3 44.7 %copy-start.8 = (bf16[512,1024]{1,0:T(8,128)(2,1)S(1)}, bf16[512,1024]{1,0:T(8,128)(2,1)}, u32[]{:S(2)}) copy-start(bf16[512,1024]{1,0:T(8,128)(2,1)} %param.21) | copy-start | bytes 3145732
  177.3 44.7 %copy-start.29 = (f32[1024]{0:T(1024)S(1)}, f32[1024]{0:T(1024)}, u32[]{:S(2)}) copy-start(f32[1024]{0:T(1024)} %param.31) | copy-start | bytes 12292
  177.3 48.2 %copy-start.32 = (f32[1024]{0:T(1024)S(1)}, f32[1024]{0:T(1024)}, u32[]{:S(2)}) copy-start(f32[1024]{0:T(1024)} %param.32) | copy-start | bytes 12292
  177.3 48.2 %copy-start.41 = (f32[1024]{0:T(1024)S(1)}, f32[1024]{0:T(1024)}, u32[]{:S(2)}) copy-start(f32[1024]{0:T(1024)} %param.33) | copy-start | bytes 12292
  177.3 51.2 %copy-start.44 = (f32[46]{0:T(128)S(1)}, f32[46]{0:T(128)}, u32[]{:S(2)}) copy-start(f32[46]{0:T(128)} %param.25) | copy-start | bytes 556
  177.3 84.4 %all-gather.7.cloned.1.call-start = ((), (), s32[]{:S(2)}) async-start(), calls=%async_computation.6 | async-start | bytes 5242880 | tf_op jit(solution)/shard_map/all_gather | solution.py:189
  227.2 71.2 %all-gather.9.cloned.1.call-start = ((), (), s32[]{:S(2)}) async-start(), calls=%async_computation.8 | async-start | bytes 5242880 | tf_op jit(solution)/shard_map/all_gather | solution.py:218
  231.1 67.3 %copy-start.50 = (f32[1024]{0:T(1024)S(1)}, f32[1024]{0:T(1024)}, u32[]{:S(2)}) copy-start(f32[1024]{0:T(1024)} %param.35) | copy-start | bytes 12292
  231.1 134.0 %reduce-scatter.9.cloned.1.call-start = ((), (), s32[]{:S(2)}) async-start(), calls=%async_computation.9 | async-start | bytes 5242880 | tf_op jit(solution)/shard_map/reduce_scatter | solution.py:225
  320.4 92.2 %reduce-scatter.7.cloned.1.call-start = ((), (), s32[]{:S(2)}) async-start(), calls=%async_computation.7 | async-start | bytes 5242880 | tf_op jit(solution)/shard_map/reduce_scatter | solution.py:199
  331.6 81.0 %copy-start.22 = (bf16[512,1024]{1,0:T(8,128)(2,1)S(1)}, bf16[512,1024]{1,0:T(8,128)(2,1)}, u32[]{:S(2)}) copy-start(bf16[512,1024]{1,0:T(8,128)(2,1)} %param.22) | copy-start | bytes 3145732
  331.6 81.0 %copy-start.40 = (f32[1024]{0:T(1024)S(1)}, f32[1024]{0:T(1024)}, u32[]{:S(2)}) copy-start(f32[1024]{0:T(1024)} %param.37) | copy-start | bytes 12292
  331.7 122.5 %all-gather.11.cloned.1.call-start = ((), (), s32[]{:S(2)}) async-start(), calls=%async_computation.10 | async-start | bytes 5242880 | tf_op jit(solution)/shard_map/all_gather | solution.py:236
  419.5 517.5 %all-reduce.5.cloned.1.call-start = ((), (), s32[]{:S(2)}) async-start(), calls=%async_computation.12 | async-start | bytes 12582912 | tf_op jit(solution)/shard_map/psum | solution.py:270
  721.9 261.0 %reduce-scatter.11.cloned.1.call-start = ((), (), s32[]{:S(2)}) async-start(), calls=%async_computation.11 | async-start | bytes 5242880 | tf_op jit(solution)/shard_map/reduce_scatter | solution.py:260
  945.0 38.0 %copy-start.35 = (f32[512]{0:T(512)S(1)}, f32[512]{0:T(512)}, u32[]{:S(2)}) copy-start(f32[512]{0:T(512)} %copy-done.34) | copy-start | bytes 6148
  945.0 40.2 %copy-start.36 = (f32[1024]{0:T(1024)S(1)}, f32[1024]{0:T(1024)}, u32[]{:S(2)}) copy-start(f32[1024]{0:T(1024)} %get-tuple-element.303) | copy-start | bytes 12292
  945.0 40.2 %copy-start.37 = (f32[1024]{0:T(1024)S(1)}, f32[1024]{0:T(1024)}, u32[]{:S(2)}) copy-start(f32[1024]{0:T(1024)} %get-tuple-element.315) | copy-start | bytes 12292
  945.0 40.2 %copy-start.38 = (f32[1024]{0:T(1024)S(1)}, f32[1024]{0:T(1024)}, u32[]{:S(2)}) copy-start(f32[1024]{0:T(1024)} %get-tuple-element.239) | copy-start | bytes 12292
  945.0 40.2 %copy-start.39 = (f32[1024]{0:T(1024)S(1)}, f32[1024]{0:T(1024)}, u32[]{:S(2)}) copy-start(f32[1024]{0:T(1024)} %get-tuple-element.245) | copy-start | bytes 12292
  945.1 83.8 %copy-start.1 = (bf16[1024,1024]{1,0:T(8,128)(2,1)S(1)}, bf16[1024,1024]{1,0:T(8,128)(2,1)}, u32[]{:S(2)}) copy-start(bf16[1024,1024]{1,0:T(8,128)(2,1)} %param.36) | copy-start | bytes 6291460
  (73 other events, 652.0 us)
Sparse Core Ops, SparseCore 0:
  13.9 37.1 all-gather.4
  177.4 44.4 reduce-scatter.4
  227.3 34.4 all-gather.6
  263.8 34.4 all-gather.8
  320.5 44.5 reduce-scatter.8
  368.0 44.5 reduce-scatter.6
  419.6 34.4 all-gather.10
  722.0 214.8 all-reduce.4
  939.4 43.4 reduce-scatter.10
where the time goes:
time: 1040 us
  waiting for transfers between devices  447 us (43%)
  matrix products  297 us (29%)
  other arithmetic  145 us (14%)
  blocking collectives  62.5 us (6%)
  local copies, waits for them, and re-layouts  51.4 us (5%)
  loops' own time  17.1 us (2%)
  between operations  16 us (2%)
    psum x1, waiting for transfers between devices, body(): lax.psum(g_w_qkv.astype(jnp.bfloat16), 'dp').astype(jnp.float32)  182 us
    dot_general x8, matrix products, masked_scores(): jnp.einsum('hqe,hke->hqk', query_block, keys, preferred_element_type=jnp....  85.5 us
    convert_element_type x4, other arithmetic, backward_block(): grad_scores = (probs * (grad_probs - jnp.sum(probs * grad_probs, axis=-1,...  60 us
    reduce_scatter x1, waiting for transfers between devices, body(): lax.psum_scatter(jnp.dot(heads_b, w_out, preferred_element_type=jnp.float...  44.6 us
    reduce_scatter x1, waiting for transfers between devices, body(): lax.psum_scatter(jnp.dot(active_b, w_down, preferred_element_type=jnp.flo...  44.5 us
    psum x1, blocking collectives, body(): lax.psum((g_ln1_gain, g_ln1_bias, g_b_out, g_ln2_gain, g_ln2_bias, g_b_do...  40 us
    dot_general x4, matrix products, backward_block(): jnp.einsum('hqe,hke->hqk', grad_block, values, preferred_element_type=jnp...  37.1 us
    all_gather x1, waiting for transfers between devices, body(): lax.all_gather(normed1_b, 'tensor', axis=0, tiled=True)  37 us
  transfers between devices with their start and end apart: 9, of which 9 were waited for; matrix products, arithmetic and copies ran while one was open for 7% of the time, Pallas kernels for 0%

commit v1 on v0

--- a/solution.py
+++ b/solution.py
@@ -267,7 +267,7 @@
     g_ln1_bias = jnp.sum(grad_norm1, axis=0)
     grad_input = grad_middle + norm_back(grad_norm1, unit1, factor1, ln1_gain)
     weights = (
-        lax.psum(g_w_qkv.astype(jnp.bfloat16), "dp").astype(jnp.float32),
+        jnp.sum(lax.all_gather(g_w_qkv.astype(jnp.bfloat16), "dp"), axis=0).astype(jnp.float32),
         lax.psum(g_b_qv.astype(jnp.bfloat16), "dp").astype(jnp.float32),
         lax.psum(g_w_out.astype(jnp.bfloat16), "dp").astype(jnp.float32),
         lax.psum(g_w_up.astype(jnp.bfloat16), "dp").astype(jnp.float32),

time: 1040 us -> 972 us (0.935)
  waiting for transfers between devices: 447 us -> 366 us
    psum x1, waiting for transfers between devices: 182 us -> 0.01 us  [body(): lax.psum(g_w_out.astype(jnp.bfloat16), 'dp').astype(jnp.float32)]
    all_gather x0 -> x1, waiting for transfers between devices: none -> 131 us  [body(): lax.all_gather(g_w_qkv.astype(jnp.bfloat16), 'dp')]
    reduce_scatter x1, waiting for transfers between devices: 35 us -> 5.12 us  [body(): lax.psum_scatter(times_trans(grad_mixed_b, w_qkv).astype(jnp.bfloat16), '...]
  transfers between devices with their start and end apart: 9 -> 10, of which waited for: 9 -> 9; matrix products, arithmetic and copies ran while one was open for 7% -> 32% of each run, Pallas kernels for 0% -> 0%
where the time goes in v1:
time: 972 us; the launch traced here: 968 us
  waiting for transfers between devices  366 us (38%)
  matrix products  300 us (31%)
  other arithmetic  155 us (16%)
  blocking collectives  63.8 us (7%)
  local copies, waits for them, and re-layouts  49.7 us (5%)
  loops' own time  17.1 us (2%)
  between operations  16.2 us (2%)
    all_gather x1, waiting for transfers between devices, body(): lax.all_gather(g_w_qkv.astype(jnp.bfloat16), 'dp')  131 us
    dot_general x8, matrix products, masked_scores(): jnp.einsum('hqe,hke->hqk', query_block, keys, preferred_element_type=jnp....  85.6 us
    convert_element_type x4, other arithmetic, backward_block(): grad_scores = (probs * (grad_probs - jnp.sum(probs * grad_probs, axis=-1,...  60.5 us
    reduce_scatter x1, waiting for transfers between devices, body(): lax.psum_scatter(jnp.dot(heads_b, w_out, preferred_element_type=jnp.float...  44.6 us
    reduce_scatter x1, waiting for transfers between devices, body(): lax.psum_scatter(jnp.dot(active_b, w_down, preferred_element_type=jnp.flo...  44.5 us
    psum x1, blocking collectives, body(): lax.psum((g_ln1_gain, g_ln1_bias, g_b_out, g_ln2_gain, g_ln2_bias, g_b_do...  42.6 us
    dot_general x4, matrix products, backward_block(): jnp.einsum('hqe,hke->hqk', grad_block, values, preferred_element_type=jnp...  37.1 us
    all_gather x1, waiting for transfers between devices, body(): lax.all_gather(normed1_b, 'tensor', axis=0, tiled=True)  37 us
  transfers between devices with their start and end apart: 10, of which 9 were waited for; matrix products, arithmetic and copies ran while one was open for 32% of the time, Pallas kernels for 0%

profile of v1, /device:TPU:0, one launch (start us, length us, event | category | flops | bytes accessed | tf_op | source)
XLA Modules:
  0.0 967.7 jit_solution(8893081762318555789)
XLA Ops:
  14.1 37.0 %all-gather.7.cloned.1.call-done = bf16[2048,1024]{1,0:T(8,128)(2,1)} async-done(((bf16[512,1024]{1,0:T(8,128)(2,1)}), bf16[2048,1024]{1,0:T(8,128)(2,1)}) %all-gather.7.cloned.1.call-update) | async-done | bytes 4194320 | tf_op jit(solution)/shard_map/all_gather | solution.py:158
  60.2 106.8 %while.48 = (s32[]{:T(128)}, bf16[4,4,512,64]{2,3,1,0:T(8,128)(2,1)}, f32[4,4,512]{2,1,0:T(4,128)S(1)}, s32[4]{0:T(128)S(1)}, s32[]{:T(128)}, /*index=5*/bf16[4,...) while((s32[]{:T(128)}, ...), condition=%wide.region_5.6_spmd.clone, body=%wide.region_2.5_spmd.clone.sunk | while | flops 1153434112 | bytes 99428696 | solution.py:74
  177.8 44.6 %reduce-scatter.5.cloned.1.call-done = bf16[512,1024]{1,0:T(8,128)(2,1)} async-done(((bf16[2048,1024]{1,0:T(8,128)(2,1)}), bf16[512,1024]{1,0:T(8,128)(2,1)}) %reduce-scatter.5.cloned.1.call-update) | async-done | bytes 1048592 | tf_op jit(solution)/shard_map/reduce_scatter | solution.py:178
  231.6 30.6 %all-gather.9.cloned.1.call-done = bf16[2048,1024]{1,0:T(8,128)(2,1)} async-done(((bf16[512,1024]{1,0:T(8,128)(2,1)}), bf16[2048,1024]{1,0:T(8,128)(2,1)}) %all-gather.9.cloned.1.call-update) | async-done | bytes 4194320 | tf_op jit(solution)/shard_map/all_gather | solution.py:189
  262.2 11.4 %fusion.83 = f32[2048,1024]{1,0:T(8,128)} fusion(bf16[2048,1024]{1,0:T(8,128)(2,1)} %all-gather.9.cloned.1.call-done, bf16[1024,1024]{1,0:T(8,128)(2,1)} %param.34), kind=kOutput, calls=%fused_computation.151 | convolution fusion | flops 4294967296 | bytes 14680064 | tf_op jit(solution)/shard_map/dot_general | solution.py:188
  273.6 25.2 %all-gather.11.cloned.1.call-done = bf16[2048,1024]{1,0:T(8,128)(2,1)} async-done(((bf16[512,1024]{1,0:T(8,128)(2,1)}), bf16[2048,1024]{1,0:T(8,128)(2,1)}) %all-gather.11.cloned.1.call-update) | async-done | bytes 4194320 | tf_op jit(solution)/shard_map/all_gather | solution.py:218
  298.8 13.5 %fusion.76 = (bf16[1024]{0:T(1024)(128)(2,1)}, bf16[2048,1024]{1,0:T(8,128)(2,1)S(1)}) fusion(f32[2048,1024]{1,0:T(8,128)} %fusion.83, f32[1024]{0:T(1024)S(1)} %copy-done.47, bf16[2048,1024]{1,0:T(8,128)(2,1)} %all-gather.11.cloned.1.call-done, bf16[1024,1024]{1,0:T(8,128)(2,1)S(1)} %copy-done), kind=kOutput, calls=%fused_computation.146 | convolution fusion | flops 4341103616 | bytes 18880512 | tf_op jit(solution)/shard_map/dot_general | solution.py:34
  320.6 11.2 %convolution_convert_fusion.3 = bf16[2048,1024]{1,0:T(8,128)(2,1)} fusion(bf16[1024,1024]{1,0:T(8,128)(2,1)S(1)} %copy-done, f32[2048,1024]{1,0:T(8,128)} %fusion.83, f32[1024]{0:T(1024)S(1)} %copy-done.47), kind=kOutput, calls=%fused_computation.65 | convolution fusion | flops 4318035968 | bytes 14684160 | tf_op jit(solution)/shard_map/dot_general | solution.py:200
  331.8 33.4 %reduce-scatter.9.cloned.1.call-done = bf16[512,1024]{1,0:T(8,128)(2,1)} async-done(((bf16[2048,1024]{1,0:T(8,128)(2,1)}), bf16[512,1024]{1,0:T(8,128)(2,1)}) %reduce-scatter.9.cloned.1.call-update) | async-done | bytes 1048592 | tf_op jit(solution)/shard_map/reduce_scatter | solution.py:225
  368.2 44.5 %reduce-scatter.7.cloned.1.call-done = bf16[512,1024]{1,0:T(8,128)(2,1)} async-done(((bf16[2048,1024]{1,0:T(8,128)(2,1)}), bf16[512,1024]{1,0:T(8,128)(2,1)}) %reduce-scatter.7.cloned.1.call-update) | async-done | bytes 1048592 | tf_op jit(solution)/shard_map/reduce_scatter | solution.py:199
  429.4 11.0 %convolution_convert_fusion.5 = bf16[1024,1024]{1,0:T(8,128)(2,1)} fusion(bf16[2048,1024]{1,0:T(8,128)(2,1)S(1)} %copy-done.44, f32[2048,1024]{1,0:T(8,128)} %fusion.83, f32[1024]{0:T(1024)S(1)} %copy-done.47), kind=kOutput, calls=%fused_computation.109 | convolution fusion | flops 4316987392 | bytes 14684160 | tf_op jit(solution)/shard_map/dot_general | solution.py:28
  440.4 14.1 %all-gather.13.cloned.1.call-done = bf16[2048,1024]{1,0:T(8,128)(2,1)} async-done(((bf16[512,1024]{1,0:T(8,128)(2,1)}), bf16[2048,1024]{1,0:T(8,128)(2,1)}) %all-gather.13.cloned.1.call-update) | async-done | bytes 4194320 | tf_op jit(solution)/shard_map/all_gather | solution.py:236
  465.2 246.0 %while.49 = (s32[]{:T(128)}, f32[4,2048,64]{1,2,0:T(8,128)}, f32[4,2048,64]{1,2,0:T(8,128)}, bf16[4,4,512,64]{2,3,1,0:T(8,128)(2,1)}, s32[4]{0:T(128)S(1)}, /*in...) while((s32[]{:T(128)}, f32[4,2048,64]{1,2,0:T(8,128)}, ...), condition=%wide.region_16.17_spmd.clone, body=%wide.region_14.16_spmd.clone.sunk | while | flops 2737439232 | bytes 296274944 | solution.py:121
  479.7 14.5 %multiply_reduce_fusion.3 = (f32[4,512]{1,0:T(4,128)S(1)}, f32[4,512,2048]{2,1,0:T(8,128)}) fusion(f32[4,512,2048]{2,1,0:T(8,128)} %fusion.148, f32[4,512]{1,0:T(4,128)S(1)} %constant_dynamic-slice_fusion.2, f32[512,2048]{1,0:T(8,128)S(1)} %subtract_convert_fusion.5, f32[4]{0:T(128)S(1)} %multiply_exponential_fusion.5, ...), kind=kOutput, calls=%fused_computation.23.clone.1 | convolution fusion | flops 566228992 | bytes 40124932 | tf_op jit(solution)/shard_map/while/body/eval_jaxpr/while/body/eval_jaxpr/hqe,hke->hqk/dot_general | solution.py:50
  494.2 15.3 %multiply_convert_fusion.5 = bf16[4,512,2048]{2,1,0:T(8,128)(2,1)} fusion(f32[4,512,2048]{2,1,0:T(8,128)} %get-tuple-element.455, f32[4,512,2048]{2,1,0:T(8,128)} %fusion.148, f32[4,512]{1,0:T(4,128)S(1)} %get-tuple-element.456), kind=kLoop, calls=%fused_computation.22.clone.1 | loop fusion | flops 12582912 | bytes 41951232 | tf_op jit(solution)/shard_map/while/body/eval_jaxpr/while/body/eval_jaxpr/convert_element_type | solution.py:99
  541.2 14.5 %multiply_reduce_fusion.3 = (f32[4,512]{1,0:T(4,128)S(1)}, f32[4,512,2048]{2,1,0:T(8,128)}) fusion(f32[4,512,2048]{2,1,0:T(8,128)} %fusion.148, f32[4,512]{1,0:T(4,128)S(1)} %constant_dynamic-slice_fusion.2, f32[512,2048]{1,0:T(8,128)S(1)} %subtract_convert_fusion.5, f32[4]{0:T(128)S(1)} %multiply_exponential_fusion.5, ...), kind=kOutput, calls=%fused_computation.23.clone.1 | convolution fusion | flops 566228992 | bytes 40124932 | tf_op jit(solution)/shard_map/while/body/eval_jaxpr/while/body/eval_jaxpr/hqe,hke->hqk/dot_general | solution.py:50
  555.8 15.1 %multiply_convert_fusion.5 = bf16[4,512,2048]{2,1,0:T(8,128)(2,1)} fusion(f32[4,512,2048]{2,1,0:T(8,128)} %get-tuple-element.455, f32[4,512,2048]{2,1,0:T(8,128)} %fusion.148, f32[4,512]{1,0:T(4,128)S(1)} %get-tuple-element.456), kind=kLoop, calls=%fused_computation.22.clone.1 | loop fusion | flops 12582912 | bytes 41951232 | tf_op jit(solution)/shard_map/while/body/eval_jaxpr/while/body/eval_jaxpr/convert_element_type | solution.py:99
  603.2 14.5 %multiply_reduce_fusion.3 = (f32[4,512]{1,0:T(4,128)S(1)}, f32[4,512,2048]{2,1,0:T(8,128)}) fusion(f32[4,512,2048]{2,1,0:T(8,128)} %fusion.148, f32[4,512]{1,0:T(4,128)S(1)} %constant_dynamic-slice_fusion.2, f32[512,2048]{1,0:T(8,128)S(1)} %subtract_convert_fusion.5, f32[4]{0:T(128)S(1)} %multiply_exponential_fusion.5, ...), kind=kOutput, calls=%fused_computation.23.clone.1 | convolution fusion | flops 566228992 | bytes 40124932 | tf_op jit(solution)/shard_map/while/body/eval_jaxpr/while/body/eval_jaxpr/hqe,hke->hqk/dot_general | solution.py:50
  617.7 15.0 %multiply_convert_fusion.5 = bf16[4,512,2048]{2,1,0:T(8,128)(2,1)} fusion(f32[4,512,2048]{2,1,0:T(8,128)} %get-tuple-element.455, f32[4,512,2048]{2,1,0:T(8,128)} %fusion.148, f32[4,512]{1,0:T(4,128)S(1)} %get-tuple-element.456), kind=kLoop, calls=%fused_computation.22.clone.1 | loop fusion | flops 12582912 | bytes 41951232 | tf_op jit(solution)/shard_map/while/body/eval_jaxpr/while/body/eval_jaxpr/convert_element_type | solution.py:99
  664.3 14.5 %multiply_reduce_fusion.3 = (f32[4,512]{1,0:T(4,128)S(1)}, f32[4,512,2048]{2,1,0:T(8,128)}) fusion(f32[4,512,2048]{2,1,0:T(8,128)} %fusion.148, f32[4,512]{1,0:T(4,128)S(1)} %constant_dynamic-slice_fusion.2, f32[512,2048]{1,0:T(8,128)S(1)} %subtract_convert_fusion.5, f32[4]{0:T(128)S(1)} %multiply_exponential_fusion.5, ...), kind=kOutput, calls=%fused_computation.23.clone.1 | convolution fusion | flops 566228992 | bytes 40124932 | tf_op jit(solution)/shard_map/while/body/eval_jaxpr/while/body/eval_jaxpr/hqe,hke->hqk/dot_general | solution.py:50
  678.8 15.0 %multiply_convert_fusion.5 = bf16[4,512,2048]{2,1,0:T(8,128)(2,1)} fusion(f32[4,512,2048]{2,1,0:T(8,128)} %get-tuple-element.455, f32[4,512,2048]{2,1,0:T(8,128)} %fusion.148, f32[4,512]{1,0:T(4,128)S(1)} %get-tuple-element.456), kind=kLoop, calls=%fused_computation.22.clone.1 | loop fusion | flops 12582912 | bytes 41951232 | tf_op jit(solution)/shard_map/while/body/eval_jaxpr/while/body/eval_jaxpr/convert_element_type | solution.py:99
  733.4 21.2 %all-reduce.1 = (bf16[512]{0:T(512)(128)(2,1)S(1)}, bf16[1024]{0:T(1024)(128)(2,1)S(1)}) all-reduce(bf16[512]{0:T(512)(128)(2,1)S(1)} %convert_element_type.192, bf16[1024]{0:T(1024)(128)(2,1)S(1)} %copy-done.42), channel_id=1, replica_groups=mesh['dp'=8,'tensor'=4] {'dp'}, use_global_device_ids=true, to_apply=%region_26.27 | all-reduce | flops 1536 | bytes 6144 | tf_op jit(solution)/shard_map/psum | solution.py:271
  772.2 42.6 %all-reduce = (f32[1024]{0:T(1024)}, f32[1024]{0:T(1024)}, f32[1024]{0:T(1024)}, f32[1024]{0:T(1024)}, f32[1024]{0:T(1024)}, /*index=5*/f32[1024]{0:T(1024)}) all-reduce(f32[1024]{0:T(1024)S(1)} %get-tuple-element.241, f32[1024]{0:T(1024)S(1)} %get-tuple-element.246, ...), channel_id=1, replica_groups=mesh['dp'=8,'tensor'=4] {'dp','tensor'}, use_global_device_ids=true, to_apply=%region_21.22 | all-reduce | flops 6144 | bytes 49152 | tf_op jit(solution)/shard_map/psum | solution.py:277
  818.4 130.9 %all-gather.15.cloned.1.call-done = bf16[8192,768]{1,0:T(8,128)(2,1)} async-done(((bf16[1024,768]{1,0:T(8,128)(2,1)}), bf16[8192,768]{1,0:T(8,128)(2,1)}) %all-gather.15.cloned.1.call-update) | async-done | bytes 12582928 | tf_op jit(solution)/shard_map/all_gather | solution.py:270
  (336 shorter events, 344.9 us)
Async XLA Ops:
  7.2 291.6 %copy-start = (bf16[1024,1024]{1,0:T(8,128)(2,1)S(1)}, bf16[1024,1024]{1,0:T(8,128)(2,1)}, u32[]{:S(2)}) copy-start(bf16[1024,1024]{1,0:T(8,128)(2,1)} %param.36) | copy-start | bytes 6291460
  7.2 43.9 %all-gather.7.cloned.1.call-start = ((), (), s32[]{:S(2)}) async-start(), calls=%async_computation.4 | async-start | bytes 5242880 | tf_op jit(solution)/shard_map/all_gather | solution.py:158
  13.8 208.6 %reduce-scatter.5.cloned.1.call-start = ((), (), s32[]{:S(2)}) async-start(), calls=%async_computation.5 | async-start | bytes 5242880 | tf_op jit(solution)/shard_map/reduce_scatter | solution.py:178
  177.7 44.7 %copy-start.8 = (bf16[512,1024]{1,0:T(8,128)(2,1)S(1)}, bf16[512,1024]{1,0:T(8,128)(2,1)}, u32[]{:S(2)}) copy-start(bf16[512,1024]{1,0:T(8,128)(2,1)} %param.21) | copy-start | bytes 3145732
  177.7 44.7 %copy-start.28 = (f32[1024]{0:T(1024)S(1)}, f32[1024]{0:T(1024)}, u32[]{:S(2)}) copy-start(f32[1024]{0:T(1024)} %param.31) | copy-start | bytes 12292
  177.7 48.3 %copy-start.31 = (f32[1024]{0:T(1024)S(1)}, f32[1024]{0:T(1024)}, u32[]{:S(2)}) copy-start(f32[1024]{0:T(1024)} %param.32) | copy-start | bytes 12292
  177.7 48.3 %copy-start.40 = (f32[1024]{0:T(1024)S(1)}, f32[1024]{0:T(1024)}, u32[]{:S(2)}) copy-start(f32[1024]{0:T(1024)} %param.33) | copy-start | bytes 12292
  177.7 51.2 %copy-start.43 = (f32[46]{0:T(128)S(1)}, f32[46]{0:T(128)}, u32[]{:S(2)}) copy-start(f32[46]{0:T(128)} %param.25) | copy-start | bytes 556
  177.7 84.5 %all-gather.9.cloned.1.call-start = ((), (), s32[]{:S(2)}) async-start(), calls=%async_computation.6 | async-start | bytes 5242880 | tf_op jit(solution)/shard_map/all_gather | solution.py:189
  227.6 71.2 %all-gather.11.cloned.1.call-start = ((), (), s32[]{:S(2)}) async-start(), calls=%async_computation.8 | async-start | bytes 5242880 | tf_op jit(solution)/shard_map/all_gather | solution.py:218
  231.5 67.3 %copy-start.47 = (f32[1024]{0:T(1024)S(1)}, f32[1024]{0:T(1024)}, u32[]{:S(2)}) copy-start(f32[1024]{0:T(1024)} %param.35) | copy-start | bytes 12292
  231.5 133.6 %reduce-scatter.9.cloned.1.call-start = ((), (), s32[]{:S(2)}) async-start(), calls=%async_computation.9 | async-start | bytes 5242880 | tf_op jit(solution)/shard_map/reduce_scatter | solution.py:225
  320.5 92.2 %reduce-scatter.7.cloned.1.call-start = ((), (), s32[]{:S(2)}) async-start(), calls=%async_computation.7 | async-start | bytes 5242880 | tf_op jit(solution)/shard_map/reduce_scatter | solution.py:199
  331.7 33.5 %copy-start.17 = (bf16[512,1024]{1,0:T(8,128)(2,1)S(1)}, bf16[512,1024]{1,0:T(8,128)(2,1)}, u32[]{:S(2)}) copy-start(bf16[512,1024]{1,0:T(8,128)(2,1)} %reduce-scatter.5.cloned.1.call-done) | copy-start | bytes 3145732
  331.7 81.0 %copy-start.22 = (bf16[512,1024]{1,0:T(8,128)(2,1)S(1)}, bf16[512,1024]{1,0:T(8,128)(2,1)}, u32[]{:S(2)}) copy-start(bf16[512,1024]{1,0:T(8,128)(2,1)} %param.22) | copy-start | bytes 3145732
  331.7 81.0 %copy-start.39 = (f32[1024]{0:T(1024)S(1)}, f32[1024]{0:T(1024)}, u32[]{:S(2)}) copy-start(f32[1024]{0:T(1024)} %param.37) | copy-start | bytes 12292
  331.8 122.7 %all-gather.13.cloned.1.call-start = ((), (), s32[]{:S(2)}) async-start(), calls=%async_computation.10 | async-start | bytes 5242880 | tf_op jit(solution)/shard_map/all_gather | solution.py:236
  419.8 336.0 %all-reduce.5.cloned.1.call-start = ((), (), s32[]{:S(2)}) async-start(), calls=%async_computation.13 | async-start | bytes 9437184 | tf_op jit(solution)/shard_map/psum | solution.py:272
  429.4 25.1 %copy-start.21 = (bf16[1,4,2048,64]{2,3,1,0:T(8,128)(2,1)S(1)}, bf16[1,4,2048,64]{2,3,1,0:T(8,128)(2,1)}, u32[]{:S(2)}) copy-start(bf16[1,4,2048,64]{2,3,1,0:T(8,128)(2,1)} %copy-done.20) | copy-start | bytes 3145732
  458.7 311.1 %reduce-scatter.11.cloned.1.call-start = ((), (), s32[]{:S(2)}) async-start(), calls=%async_computation.11 | async-start | bytes 5242880 | tf_op jit(solution)/shard_map/reduce_scatter | solution.py:260
  494.2 19.4 %copy-start.13 = (f32[4,2048,64]{1,2,0:T(8,128)S(1)}, f32[4,2048,64]{1,2,0:T(8,128)}, u32[]{:S(2)}) copy-start(f32[4,2048,64]{1,2,0:T(8,128)} %get-tuple-element.510) | copy-start | bytes 6291460 | tf_op jit(solution)/shard_map/while/body/eval_jaxpr/while
  555.8 19.8 %copy-start.13 = (f32[4,2048,64]{1,2,0:T(8,128)S(1)}, f32[4,2048,64]{1,2,0:T(8,128)}, u32[]{:S(2)}) copy-start(f32[4,2048,64]{1,2,0:T(8,128)} %get-tuple-element.510) | copy-start | bytes 6291460 | tf_op jit(solution)/shard_map/while/body/eval_jaxpr/while
  678.8 19.0 %copy-start.13 = (f32[4,2048,64]{1,2,0:T(8,128)S(1)}, f32[4,2048,64]{1,2,0:T(8,128)}, u32[]{:S(2)}) copy-start(f32[4,2048,64]{1,2,0:T(8,128)} %get-tuple-element.510) | copy-start | bytes 6291460 | tf_op jit(solution)/shard_map/while/body/eval_jaxpr/while
  725.3 224.0 %all-gather.15.cloned.1.call-start = ((), (), s32[]{:S(2)}) async-start(), calls=%async_computation.12 | async-start | bytes 14155776 | tf_op jit(solution)/shard_map/all_gather | solution.py:270
  (71 other events, 478.6 us)
Sparse Core Ops, SparseCore 0:
  13.9 37.1 all-gather.6
  177.8 44.5 reduce-scatter.4
  227.7 34.4 all-gather.8
  264.3 34.4 all-gather.10
  320.6 44.5 reduce-scatter.8
  368.1 44.5 reduce-scatter.6
  420.0 34.4 all-gather.12
  459.5 170.3 all-reduce.4
  725.4 44.3 reduce-scatter.10
  771.9 177.3 all-gather.14
